TPU v7x, 32 devices: a whole 2x2x4 slice. The times are simulated.
32 devices in a mesh: tm: 2 (over x), space: 16 (over z, y, core).
Axes of the slice: x: 2, y: 2, z: 4, core: 2. Of those that a mesh axis runs over, the one named last changes fastest.
Arguments:
- increment: float32 [4, 5, 48, 128, 128], P('tm', None, None, 'space'), may hold values from -6 to 6
- multiplier: float32 [4, 5, 48, 128, 128], P('tm', None, None, 'space'), may hold values from -20 to 20
- sensor_multiplier: float32 [4, 2048], P('tm'), may hold values from -6 to 6
- misfit: float32 [4, 5, 48, 128, 128], P('tm', None, None, 'space'), may hold values from -20 to 20
- innovation: float32 [4, 2048], P('tm'), may hold values from -6 to 6
- model_error: float32 [5, 48], replicated, may hold values from 0.2 to 1
- sensor_error: float32 [4, 2048], P('tm'), may hold values from 0.3 to 1.5
- trajectory: bfloat16 [4, 2, 2, 48, 128, 128], P('tm', None, None, None, 'space'), may hold values from 0 to 1
- land_sea: int32 [128, 128], P('space'), may hold values 0 or 1
- sensor_cells: int32 [4, 2048], P('tm'), may hold values from 0 to 1572863
Outputs:
- increment_next: float32 [4, 5, 48, 128, 128], P('tm', None, None, 'space')
- multiplier_next: float32 [4, 5, 48, 128, 128], P('tm', None, None, 'space')
- sensor_next: float32 [4, 2048], P('tm')
Inputs may be any that keep to these rules, and one draw needn't show every extreme that they name: `sensor_cells`: the flat index ((f * 48 + l) * 128 + x) * 128 + y of the observed cell at field f (0 temperature, 1 salinity), level l, column x, row y; an index may repeat.
All inputs are finite; a program needn't handle non-finite values. No bound on the sum of `land_sea` on one device may be relied on, other than what follows from the above.
Results may differ from a plain program's by a relative error of at most 0.0017.
Values may be sent and summed in bfloat16 or wider, within the bound.
No kernel may reach another device: no remote copies, remote signals or barrier semaphores. Data moves between devices by JAX's collectives and lax.ppermute only.
A program may use at most 64 MiB of HBM per device.

v0:
```python
import jax
import jax.numpy as jnp
from jax import lax
from jax.sharding import PartitionSpec as P

thermal_lin = 0.2
thermal_quad = 0.02
haline_lin = 0.8
cabbeling = 0.01
gravity = 1.0
time_stride = 0.3
mixing = 0.15
coriolis = 0.5
relaxation = 0.5
epsilon = 1e-06


def extended(shard, sides, width):
    for axis, dim in sides:
        peers, length = (lax.axis_size(axis), shard.shape[dim])
        up = [(i, (i + 1) % peers) for i in range(peers)]
        down = [(j, i) for i, j in up]
        last = lax.slice_in_dim(shard, length - width, length, axis=dim)
        first = lax.slice_in_dim(shard, 0, width, axis=dim)
        before = lax.ppermute(last, axis, up)
        after = lax.ppermute(first, axis, down)
        shard = jnp.concatenate([before, shard, after], axis=dim)
    return shard


def shifted(shard, axis, by):
    peers = lax.axis_size(axis)
    pairs = [(i, i + by) for i in range(peers) if 0 <= i + by < peers]
    return lax.ppermute(shard, axis, pairs)


def column_pad(values):
    return jnp.pad(values, ((0, 0), (0, 0), (1, 1)))


def tendency(padded, history, landmask):
    temper = 30.0 * history[0] - 10.0
    saline = 8.0 * history[1] - 5.0
    dens_temper = -thermal_lin - thermal_quad * temper + cabbeling * saline
    dens_saline = haline_lin + cabbeling * temper
    density = dens_temper * padded[0] + dens_saline * padded[1]
    pressure = padded[4] + gravity * density
    latitude = padded.shape[3]
    rotation = (
        coriolis
        * (jnp.arange(latitude, dtype=jnp.float32) - 0.5 * (latitude - 1))
        / (0.5 * latitude)
    )

    def middle(f):
        return f[:, 1:-1]

    def zonal_slope(f):
        return 0.5 * (f[:, 2:] - f[:, :-2])

    def meridional_slope(f):
        g = column_pad(middle(f))
        return 0.5 * (g[..., 2:] - g[..., :-2])

    def laplacian(f):
        g = column_pad(middle(f))
        return f[:, 2:] + f[:, :-2] + g[..., 2:] + g[..., :-2] - 4.0 * middle(f)

    heat_next = middle(padded[0]) + mixing * laplacian(padded[0])
    salt_next = middle(padded[1]) + mixing * laplacian(padded[1])
    east_next = middle(padded[2]) + time_stride * (
        rotation * middle(padded[3]) - zonal_slope(pressure)
    )
    north_next = middle(padded[3]) + time_stride * (
        -rotation * middle(padded[2]) - meridional_slope(pressure)
    )
    surface_next = (
        middle(padded[4])
        - time_stride * (zonal_slope(padded[2]) + meridional_slope(padded[3]))
        + mixing * laplacian(padded[4])
    )
    return jnp.stack([heat_next, salt_next, east_next, north_next, surface_next]) * landmask


def tangent_substep(fields, history, landmask):
    padded = extended(fields, (("space", 2),), 1)
    return tendency(padded, history, landmask)


def adjoint_substep(upstream, history, landmask):
    blank = jnp.zeros(
        upstream.shape[:2] + (upstream.shape[2] + 2,) + upstream.shape[3:], jnp.float32
    )
    _, pull = jax.vjp(lambda v: tendency(v, history, landmask), blank)
    spread = pull(upstream)[0]
    rims = jnp.concatenate([spread[:, :, :1], spread[:, :, -1:]], axis=2)
    beyond = extended(rims.astype(jnp.bfloat16), (("space", 2),), 1).astype(rims.dtype)
    inner = spread[:, :, 1:-1]
    inner = inner.at[:, :, 0].add(beyond[:, :, 0])
    inner = inner.at[:, :, -1].add(beyond[:, :, 3])
    return inner


def on_device(
    increment,
    multiplier,
    sensor_multiplier,
    misfit,
    innovation,
    model_error,
    sensor_error,
    trajectory,
    land_sea,
    sensor_cells,
):
    subcount = increment.shape[0]
    substeps = trajectory.shape[1]
    levels = increment.shape[2]
    width = increment.shape[3]
    latitude = increment.shape[4]
    landmask = land_sea.astype(jnp.float32)
    forward = []
    history = extended(trajectory, (("space", 4),), 1).astype(jnp.float32)
    for k in range(subcount):
        fields = increment[k]
        for j in range(substeps):
            fields = tangent_substep(fields, history[k, j], landmask)
        forward.append(fields)
    damping = model_error[:, :, None, None]
    partial_value = multiplier[0] + relaxation * (
        misfit[0] - damping * multiplier[0] - increment[0]
    )
    received = shifted(partial_value, "tm", -1)
    incoming = shifted(forward[-1].astype(jnp.bfloat16), "tm", 1).astype(jnp.float32)
    previous = jnp.stack([incoming] + forward[:-1])
    model_residual = misfit - damping[None] * multiplier - (increment - previous)
    multiplier_next = multiplier + relaxation * model_residual
    columns = width * lax.axis_size("space")
    plane = columns * latitude
    offset = lax.axis_index("space") * width
    field_level = sensor_cells // plane
    remainder = sensor_cells % plane
    column_index = remainder // latitude
    row_index = remainder % latitude
    owned = (column_index >= offset) & (column_index < offset + width)
    local_index = jnp.where(
        owned, (field_level * width + (column_index - offset)) * latitude + row_index, 0
    )
    flattened = increment[:, :2].reshape(subcount, 2 * levels * width * latitude)
    local_values = jnp.where(owned, jnp.take_along_axis(flattened, local_index, axis=1), 0.0)
    observed = lax.psum(local_values, "space")
    sensor_residual = innovation - sensor_error * sensor_multiplier - observed
    sensor_next = sensor_multiplier + relaxation * sensor_residual
    misfit_local = jnp.sum(model_residual * model_residual) + jnp.sum(
        jnp.where(owned, sensor_residual * sensor_residual, 0.0)
    )
    misfit_square = lax.psum(misfit_local, ("tm", "space"))
    keeper = jnp.where(lax.axis_index("tm") < lax.axis_size("tm") - 1, 1.0, 0.0).astype(jnp.float32)
    carried = keeper * (received + relaxation * forward[-1])
    following = [multiplier_next[1]] + [carried]
    returned = []
    for k in range(subcount):
        upstream = following[k]
        for j in reversed(range(substeps)):
            upstream = adjoint_substep(upstream, history[k, j], landmask)
        returned.append(upstream)
    returned = jnp.stack(returned)
    subwindow_rows = jnp.arange(subcount, dtype=jnp.int32)[:, None]
    spread = (
        jnp.zeros_like(flattened)
        .at[subwindow_rows, local_index]
        .add(jnp.where(owned, sensor_next, 0.0))
    )
    spread = spread.reshape(subcount, 2, levels, width, latitude)
    sensor_part = jnp.concatenate(
        [spread, jnp.zeros((subcount, 3, levels, width, latitude), jnp.float32)], axis=1
    )
    gradient = multiplier_next - returned + sensor_part
    gradient_local = jnp.sum(gradient * gradient)
    gradient_square = lax.psum(gradient_local, ("tm", "space"))
    stride = misfit_square / (gradient_square + epsilon)
    return (increment - stride * gradient, multiplier_next, sensor_next)


def solution(mesh):
    placed = (
        P("tm", None, None, "space", None),
        P("tm", None, None, "space", None),
        P("tm", None),
        P("tm", None, None, "space", None),
        P("tm", None),
        P(),
        P("tm", None),
        P("tm", None, None, None, "space", None),
        P("space", None),
        P("tm", None),
    )
    return jax.shard_map(
        on_device,
        mesh=mesh,
        in_specs=placed,
        out_specs=(
            P("tm", None, None, "space", None),
            P("tm", None, None, "space", None),
            P("tm", None),
        ),
        check_vma=False,
    )
```

profile of v0, /device:TPU:12, one launch (start us, length us, event | category | flops | bytes accessed | tf_op | source)
XLA Modules:
  0.0 275.0 jit_solution(7733373252977561746)
XLA Ops:
  0.6 1.9 copy.36
  4.5 1.7 collective-permute-start.1
  7.2 2.6 collective-permute-start.2
  10.7 34.9 %gather_fusion = f32[4096]{0:T(1024)S(1)} fusion(f32[2,98304]{1,0:T(2,128)S(1)} %bitcast.526, s32[4096]{0:T(1024)S(1)} %bitcast.527), kind=kCustom, calls=%fused_computation | custom fusion | bytes 65536 | tf_op jit(solution)/shard_map/jit(take_along_axis)/gather | solution.py:150
  45.7 50.0 %psum.21 = f32[2,2048]{1,0:T(2,128)S(1)} all-reduce(f32[2,2048]{1,0:T(2,128)S(1)} %fusion.203), channel_id=1, replica_groups=mesh['tm'=2,'space'=16] {'space'}, use_global_device_ids=true, to_apply=%region_1.2 | all-reduce | flops 4096 | bytes 32768 | tf_op jit(solution)/shard_map/psum | solution.py:151
  95.6 1.3 select_bitcast_fusion.1
  97.2 27.9 %scatter_custom_fusion = f32[196608]{0:T(1024)} fusion(s32[4096]{0:T(1024)S(1)} %bitcast.541, f32[4096]{0:T(1024)S(1)} %bitcast.540, f32[]{:T(128)} %constant.307.clone.1), kind=kCustom, calls=%fused_computation.80 | custom fusion | flops 4096 | bytes 786436
  127.0 1.1 pad_maximum_fusion
  131.9 4.5 %collective-permute-start.5 = (f32[5,48,1,128]{3,1,2,0:T(8,128)S(1)}, f32[5,48,1,128]{3,1,2,0:T(8,128)S(1)}, u32[]{:S(2)}, u32[]{:S(2)}) collective-permute-start(f32[5,48,1,128]{3,1,2,0:T(8,128)S(1)} %get-tuple-element.230), channel_id=1, source_target_pairs={{1,0},{2,1},{3,2},{4,3},{5,4},{6,5},{7,6},{8,7},{9,8},{10,9},{11,1... | collective-permute-start | bytes 368648 | tf_op jit(solution)/shard_map/ppermute | solution.py:26
  137.1 2.9 %collective-permute-done.4 = f32[5,48,1,128]{3,1,2,0:T(8,128)S(1)} collective-permute-done((f32[5,48,1,128]{3,1,2,0:T(8,128)S(1)}, f32[5,48,1,128]{3,1,2,0:T(8,128)S(1)}, u32[]{:S(2)}, u32[]{:S(2)}) %collective-permute-start.4) | collective-permute-done | bytes 122912 | tf_op jit(solution)/shard_map/ppermute | solution.py:25
  140.2 4.0 %collective-permute-done.9 = f32[5,48,1,128]{3,1,2,0:T(8,128)S(1)} collective-permute-done((f32[5,48,1,128]{3,1,2,0:T(8,128)S(1)}, f32[5,48,1,128]{3,1,2,0:T(8,128)S(1)}, u32[]{:S(2)}, u32[]{:S(2)}) %collective-permute-start.9) | collective-permute-done | bytes 122912 | tf_op jit(solution)/shard_map/ppermute | solution.py:25
  145.7 4.3 %collective-permute-start.6 = (bf16[5,48,8,128]{3,1,2,0:T(8,128)(2,1)S(1)}, bf16[5,48,8,128]{3,1,2,0:T(8,128)(2,1)S(1)}, u32[]{:S(2)}, u32[]{:S(2)}) collective-permute-start(bf16[5,48,8,128]{3,1,2,0:T(8,128)(2,1)S(1)} %multiply_convert_fusion), channel_id=1, source_target_pairs={{0,16},{1,17},{2,18},{3,19},{4,20},{5,21},{6,22},{7,23},{8,24},{9,... | collective-permute-start | bytes 1474568 | tf_op jit(solution)/shard_map/ppermute | solution.py:34
  151.1 5.0 %collective-permute-done.6 = bf16[5,48,8,128]{3,1,2,0:T(8,128)(2,1)S(1)} collective-permute-done((bf16[5,48,8,128]{3,1,2,0:T(8,128)(2,1)S(1)}, bf16[5,48,8,128]{3,1,2,0:T(8,128)(2,1)S(1)}, u32[]{:S(2)}, u32[]{:S(2)}) %collective-permute-start.6) | collective-permute-done | bytes 491552 | tf_op jit(solution)/shard_map/ppermute | solution.py:34
  156.2 1.6 broadcast_multiply_fusion
  160.3 1.4 copy-done.4
  161.8 1.2 fusion.5
  163.0 1.3 collective-permute-start.15
  165.8 1.7 collective-permute-start.12
  167.5 1.2 multiply_reduce_fusion.1
  171.1 1.6 fusion.200
  172.7 1.6 fusion.199
  174.2 8.5 %collective-permute-done.15 = f32[5,48,8,128]{3,1,2,0:T(8,128)} collective-permute-done((f32[5,48,8,128]{3,1,2,0:T(8,128)}, f32[5,48,8,128]{3,1,2,0:T(8,128)}, u32[]{:S(2)}, u32[]{:S(2)}) %collective-permute-start.15) | collective-permute-done | bytes 983072 | tf_op jit(solution)/shard_map/ppermute | solution.py:34
  182.7 1.7 broadcast_multiply_fusion.3
  188.1 1.7 collective-permute-start.17
  190.4 7.8 %collective-permute-start.13 = (bf16[5,48,1,128]{3,1,2,0:T(8,128)(2,1)S(1)}, bf16[5,48,1,128]{3,1,2,0:T(8,128)(2,1)S(1)}, u32[]{:S(2)}, u32[]{:S(2)}) collective-permute-start(bf16[5,48,1,128]{3,1,2,0:T(8,128)(2,1)S(1)} %get-tuple-element.239), channel_id=1, source_target_pairs={{0,1},{1,2},{2,3},{3,4},{4,5},{5,6},{6,7},{7,8},{8,9},{9,10},{10,1... | collective-permute-start | bytes 184328 | tf_op jit(solution)/shard_map/ppermute | solution.py:25
  199.1 2.5 collective-permute-done.14
  203.2 4.1 %collective-permute-start.18 = (bf16[5,48,1,128]{3,1,0,2:T(8,128)(2,1)S(1)}, bf16[5,48,1,128]{3,1,0,2:T(8,128)(2,1)S(1)}, u32[]{:S(2)}, u32[]{:S(2)}) collective-permute-start(bf16[5,48,1,128]{3,1,0,2:T(8,128)(2,1)S(1)} %get-tuple-element.243), channel_id=1, source_target_pairs={{0,1},{1,2},{2,3},{3,4},{4,5},{5,6},{6,7},{7,8},{8,9},{9,10},{10,1... | collective-permute-start | bytes 184328 | tf_op jit(solution)/shard_map/ppermute | solution.py:25
  209.2 1.3 copy.43
  210.5 4.4 %scatter-add.54 = f32[1,5,48,8,128]{4,3,2,1,0:T(8,128)} dynamic-update-slice(f32[1,5,48,8,128]{4,3,2,1,0:T(8,128)} %copy.43, f32[1,5,48,1,128]{4,3,2,1,0:T(1,128)S(1)} %bitcast.537, s32[]{:T(128)} %constant.322.clone.1, s32[]{:T(128)} %constant.322.clone.1, s32[]{:T(128)} %constant.322.clone.1, s32[]{:T(128)} %constant.327.clone.1, s32[]{:T(128)} %constant.322.clone.1) | dynamic-update-slice | bytes 245764 | tf_op jit(solution)/shard_map/scatter-add | solution.py:100
  214.9 2.6 multiply_reduce_fusion
  217.4 52.7 %all-reduce.221 = (f32[]{:T(128)}, f32[]{:T(128)}) all-reduce(f32[]{:T(128)S(6)} %add.910, f32[]{:T(128)} %multiply_reduce_fusion), channel_id=1, replica_groups=mesh['tm'=2,'space'=16] {'tm','space'}, use_global_device_ids=true, to_apply=%region_3.4 | all-reduce | flops 2 | bytes 16 | tf_op jit(solution)/shard_map/psum | solution.py:157
  271.4 3.6 %multiply_subtract_fusion = f32[2,5,48,8,128]{4,3,2,1,0:T(8,128)} fusion(f32[2,5,48,8,128]{4,3,2,1,0:T(8,128)} %param.26, f32[]{:T(128)S(6)} %div.69, f32[2,2,48,8,128]{4,3,2,1,0:T(8,128)} %bitcast.530, f32[2,5,48,8,128]{4,3,2,1,0:T(8,128)S(1)} %copy-done.1, f32[1,5,48,8,128]{4,3,2,1,0:T(8,128)} %scatter-add.54, f32[1,5,48,8,128]{4,3,2,1,0:T(8,128)S(1)} %copy.44), kind=kLoop, calls=%fused_computation.7 | loop fusion | flops 2457600 | bytes 8650756 | tf_op jit(solution)/shard_map/sub | solution.py:182
  (251 shorter events, 25.7 us)
Async XLA Ops:
  3.8 3.3 %copy-start.8 = (f32[5,48,8,128]{3,1,2,0:T(8,128)}, f32[5,48,8,128]{3,1,2,0:T(8,128)S(1)}, u32[]{:S(2)}) copy-start(f32[5,48,8,128]{3,1,2,0:T(8,128)S(1)} %get-tuple-element.131) | copy-start | bytes 2949124
  4.5 122.4 %collective-permute-start = (f32[5,48,1,128]{3,1,2,0:T(8,128)}, f32[5,48,1,128]{3,1,2,0:T(8,128)}, u32[]{:S(2)}, u32[]{:S(2)}) collective-permute-start(f32[5,48,1,128]{3,1,2,0:T(8,128)} %get-tuple-element.231), channel_id=1, source_target_pairs={{0,1},{1,2},{2,3},{3,4},{4,5},{5,6},{6,7},{7,8},{8,9},{9,10},{10,1... | collective-permute-start | bytes 368648 | tf_op jit(solution)/shard_map/ppermute | solution.py:25
  4.5 122.4 %collective-permute-start.1 = (f32[5,48,1,128]{3,1,2,0:T(8,128)}, f32[5,48,1,128]{3,1,2,0:T(8,128)}, u32[]{:S(2)}, u32[]{:S(2)}) collective-permute-start(f32[5,48,1,128]{3,1,2,0:T(8,128)} %get-tuple-element.232), channel_id=1, source_target_pairs={{1,0},{2,1},{3,2},{4,3},{5,4},{6,5},{7,6},{8,7},{9,8},{10,9},{11,1... | collective-permute-start | bytes 368648 | tf_op jit(solution)/shard_map/ppermute | solution.py:26
  7.0 121.1 %collective-permute-start.7 = (f32[5,48,1,128]{3,1,2,0:T(8,128)}, f32[5,48,1,128]{3,1,2,0:T(8,128)}, u32[]{:S(2)}, u32[]{:S(2)}) collective-permute-start(f32[5,48,1,128]{3,1,2,0:T(8,128)} %get-tuple-element.235), channel_id=1, source_target_pairs={{0,1},{1,2},{2,3},{3,4},{4,5},{5,6},{6,7},{7,8},{8,9},{9,10},{10,1... | collective-permute-start | bytes 368648 | tf_op jit(solution)/shard_map/ppermute | solution.py:25
  7.2 118.0 %collective-permute-start.2 = (bf16[2,2,2,48,1,128]{5,3,4,2,1,0:T(8,128)(2,1)S(1)}, bf16[2,2,2,48,1,128]{5,3,4,2,1,0:T(8,128)(2,1)S(1)}, u32[]{:S(2)}, u32[]{:S(2)}) collective-permute-start(bf16[2,2,2,48,1,128]{5,3,4,2,1,0:T(8,128)(2,1)S(1)} %get-tuple-element.237), channel_id=1, source_target_pairs={{0,1},{1,2},{2,3},{3,4},{4,5},{5,6},{6,7},{7,8},{8,9},{9,10},{10,1... | collective-permute-start | bytes 294920 | tf_op jit(solution)/shard_map/ppermute | solution.py:25
  9.8 116.0 %collective-permute-start.3 = (bf16[2,2,2,48,1,128]{5,3,4,2,1,0:T(8,128)(2,1)S(1)}, bf16[2,2,2,48,1,128]{5,3,4,2,1,0:T(8,128)(2,1)}, u32[]{:S(2)}, u32[]{:S(2)}) collective-permute-start(bf16[2,2,2,48,1,128]{5,3,4,2,1,0:T(8,128)(2,1)S(1)} %get-tuple-element.238), channel_id=1, source_target_pairs={{1,0},{2,1},{3,2},{4,3},{5,4},{6,5},{7,6},{8,7},{9,8},{10,9},{11,1... | collective-permute-start | bytes 294920 | tf_op jit(solution)/shard_map/ppermute | solution.py:26
  10.6 85.0 %copy-start.15 = (f32[2,2048]{1,0:T(2,128)S(1)}, f32[2,2048]{1,0:T(2,128)}, u32[]{:S(2)}) copy-start(f32[2,2048]{1,0:T(2,128)} %param.28) | copy-start | bytes 49156
  10.7 85.0 %copy-start.16 = (f32[2,2048]{1,0:T(2,128)S(1)}, f32[2,2048]{1,0:T(2,128)}, u32[]{:S(2)}) copy-start(f32[2,2048]{1,0:T(2,128)} %param.30) | copy-start | bytes 49156
  10.7 85.0 %copy-start.17 = (f32[2,2048]{1,0:T(2,128)S(1)}, f32[2,2048]{1,0:T(2,128)}, u32[]{:S(2)}) copy-start(f32[2,2048]{1,0:T(2,128)} %param.32) | copy-start | bytes 49156
  10.7 86.3 %copy-start.20 = (s32[2]{0:T(128)S(1)}, s32[2]{0:T(128)}, u32[]{:S(2)}) copy-start(s32[2]{0:T(128)} %constant.788) | copy-start | bytes 28
  10.7 86.4 %copy-start.21 = (s32[2]{0:T(128)S(1)}, s32[2]{0:T(128)}, u32[]{:S(2)}) copy-start(s32[2]{0:T(128)} %constant.791) | copy-start | bytes 28
  125.2 3.0 %collective-permute-start.8 = (f32[5,48,1,128]{3,1,2,0:T(8,128)}, f32[5,48,1,128]{3,1,2,0:T(8,128)S(1)}, u32[]{:S(2)}, u32[]{:S(2)}) collective-permute-start(f32[5,48,1,128]{3,1,2,0:T(8,128)} %get-tuple-element.236), channel_id=1, source_target_pairs={{1,0},{2,1},{3,2},{4,3},{5,4},{6,5},{7,6},{8,7},{9,8},{10,9},{11,1... | collective-permute-start | bytes 368648 | tf_op jit(solution)/shard_map/ppermute | solution.py:26
  131.9 8.1 %collective-permute-start.4 = (f32[5,48,1,128]{3,1,2,0:T(8,128)S(1)}, f32[5,48,1,128]{3,1,2,0:T(8,128)S(1)}, u32[]{:S(2)}, u32[]{:S(2)}) collective-permute-start(f32[5,48,1,128]{3,1,2,0:T(8,128)S(1)} %get-tuple-element.229), channel_id=1, source_target_pairs={{0,1},{1,2},{2,3},{3,4},{4,5},{5,6},{6,7},{7,8},{8,9},{9,10},{10,1... | collective-permute-start | bytes 368648 | tf_op jit(solution)/shard_map/ppermute | solution.py:25
  131.9 8.0 %collective-permute-start.5 = (f32[5,48,1,128]{3,1,2,0:T(8,128)S(1)}, f32[5,48,1,128]{3,1,2,0:T(8,128)S(1)}, u32[]{:S(2)}, u32[]{:S(2)}) collective-permute-start(f32[5,48,1,128]{3,1,2,0:T(8,128)S(1)} %get-tuple-element.230), channel_id=1, source_target_pairs={{1,0},{2,1},{3,2},{4,3},{5,4},{6,5},{7,6},{8,7},{9,8},{10,9},{11,1... | collective-permute-start | bytes 368648 | tf_op jit(solution)/shard_map/ppermute | solution.py:26
  136.5 3.7 %collective-permute-start.10 = (f32[5,48,1,128]{3,1,2,0:T(8,128)S(1)}, f32[5,48,1,128]{3,1,2,0:T(8,128)S(1)}, u32[]{:S(2)}, u32[]{:S(2)}) collective-permute-start(f32[5,48,1,128]{3,1,2,0:T(8,128)S(1)} %get-tuple-element.234), channel_id=1, source_target_pairs={{1,0},{2,1},{3,2},{4,3},{5,4},{6,5},{7,6},{8,7},{9,8},{10,9},{11,1... | collective-permute-start | bytes 368648 | tf_op jit(solution)/shard_map/ppermute | solution.py:26
  137.1 7.1 %collective-permute-start.9 = (f32[5,48,1,128]{3,1,2,0:T(8,128)S(1)}, f32[5,48,1,128]{3,1,2,0:T(8,128)S(1)}, u32[]{:S(2)}, u32[]{:S(2)}) collective-permute-start(f32[5,48,1,128]{3,1,2,0:T(8,128)S(1)} %get-tuple-element.233), channel_id=1, source_target_pairs={{0,1},{1,2},{2,3},{3,4},{4,5},{5,6},{6,7},{7,8},{8,9},{9,10},{10,1... | collective-permute-start | bytes 368648 | tf_op jit(solution)/shard_map/ppermute | solution.py:25
  145.7 10.4 %collective-permute-start.6 = (bf16[5,48,8,128]{3,1,2,0:T(8,128)(2,1)S(1)}, bf16[5,48,8,128]{3,1,2,0:T(8,128)(2,1)S(1)}, u32[]{:S(2)}, u32[]{:S(2)}) collective-permute-start(bf16[5,48,8,128]{3,1,2,0:T(8,128)(2,1)S(1)} %multiply_convert_fusion), channel_id=1, source_target_pairs={{0,16},{1,17},{2,18},{3,19},{4,20},{5,21},{6,22},{7,23},{8,24},{9,... | collective-permute-start | bytes 1474568 | tf_op jit(solution)/shard_map/ppermute | solution.py:34
  150.4 5.7 %copy-start.11 = (f32[2,5,48,8,128]{4,3,2,1,0:T(8,128)S(1)}, f32[2,5,48,8,128]{4,3,2,1,0:T(8,128)}, u32[]{:S(2)}) copy-start(f32[2,5,48,8,128]{4,3,2,1,0:T(8,128)} %param.29) | copy-start | bytes 5898244
  150.7 5.5 %copy-start.5 = (f32[2,5,48,8,128]{4,3,2,1,0:T(8,128)S(1)}, f32[2,5,48,8,128]{4,3,2,1,0:T(8,128)}, u32[]{:S(2)}) copy-start(f32[2,5,48,8,128]{4,3,2,1,0:T(8,128)} %param.27) | copy-start | bytes 5898244
  151.0 5.2 %copy-start.2 = (f32[2,5,48,8,128]{4,3,2,1,0:T(8,128)S(1)}, f32[2,5,48,8,128]{4,3,2,1,0:T(8,128)}, u32[]{:S(2)}) copy-start(f32[2,5,48,8,128]{4,3,2,1,0:T(8,128)} %param.26) | copy-start | bytes 5898244
  151.1 5.1 %copy-start.14 = (f32[5,48]{1,0:T(8,128)S(1)}, f32[5,48]{1,0:T(8,128)}, u32[]{:S(2)}) copy-start(f32[5,48]{1,0:T(8,128)} %param.31) | copy-start | bytes 2884
  163.0 19.7 %collective-permute-start.15 = (f32[5,48,8,128]{3,1,2,0:T(8,128)}, f32[5,48,8,128]{3,1,2,0:T(8,128)}, u32[]{:S(2)}, u32[]{:S(2)}) collective-permute-start(f32[5,48,8,128]{3,1,2,0:T(8,128)} %fusion.5), channel_id=1, source_target_pairs={{16,0},{17,1},{18,2},{19,3},{20,4},{21,5},{22,6},{23,7},{24,8},{25... | collective-permute-start | bytes 2949128 | tf_op jit(solution)/shard_map/ppermute | solution.py:34
  165.7 4.0 %copy-start.10 = (f32[5,48,10,128]{3,1,2,0:T(8,128)}, f32[5,48,10,128]{3,1,2,0:T(8,128)S(1)}, u32[]{:S(2)}) copy-start(f32[5,48,10,128]{3,1,2,0:T(8,128)S(1)} %get-tuple-element.106) | copy-start | bytes 3686404
  165.7 5.3 %collective-permute-start.11 = (bf16[5,48,1,128]{3,1,2,0:T(8,128)(2,1)S(1)}, bf16[5,48,1,128]{3,1,2,0:T(8,128)(2,1)S(1)}, u32[]{:S(2)}, u32[]{:S(2)}) collective-permute-start(bf16[5,48,1,128]{3,1,2,0:T(8,128)(2,1)S(1)} %get-tuple-element.241), channel_id=1, source_target_pairs={{0,1},{1,2},{2,3},{3,4},{4,5},{5,6},{6,7},{7,8},{8,9},{9,10},{10,1... | collective-permute-start | bytes 184328 | tf_op jit(solution)/shard_map/ppermute | solution.py:25
  165.8 5.3 %collective-permute-start.12 = (bf16[5,48,1,128]{3,1,2,0:T(8,128)(2,1)S(1)}, bf16[5,48,1,128]{3,1,2,0:T(8,128)(2,1)S(1)}, u32[]{:S(2)}, u32[]{:S(2)}) collective-permute-start(bf16[5,48,1,128]{3,1,2,0:T(8,128)(2,1)S(1)} %get-tuple-element.242), channel_id=1, source_target_pairs={{1,0},{2,1},{3,2},{4,3},{5,4},{6,5},{7,6},{8,7},{9,8},{10,9},{11,1... | collective-permute-start | bytes 184328 | tf_op jit(solution)/shard_map/ppermute | solution.py:26
  188.1 10.2 %collective-permute-start.16 = (bf16[5,48,1,128]{3,1,2,0:T(8,128)(2,1)S(1)}, bf16[5,48,1,128]{3,1,2,0:T(8,128)(2,1)S(1)}, u32[]{:S(2)}, u32[]{:S(2)}) collective-permute-start(bf16[5,48,1,128]{3,1,2,0:T(8,128)(2,1)S(1)} %get-tuple-element.245), channel_id=1, source_target_pairs={{0,1},{1,2},{2,3},{3,4},{4,5},{5,6},{6,7},{7,8},{8,9},{9,10},{10,1... | collective-permute-start | bytes 184328 | tf_op jit(solution)/shard_map/ppermute | solution.py:25
  188.1 10.3 %collective-permute-start.17 = (bf16[5,48,1,128]{3,1,2,0:T(8,128)(2,1)S(1)}, bf16[5,48,1,128]{3,1,2,0:T(8,128)(2,1)S(1)}, u32[]{:S(2)}, u32[]{:S(2)}) collective-permute-start(bf16[5,48,1,128]{3,1,2,0:T(8,128)(2,1)S(1)} %get-tuple-element.246), channel_id=1, source_target_pairs={{1,0},{2,1},{3,2},{4,3},{5,4},{6,5},{7,6},{8,7},{9,8},{10,9},{11,1... | collective-permute-start | bytes 184328 | tf_op jit(solution)/shard_map/ppermute | solution.py:26
  190.4 8.7 %collective-permute-start.13 = (bf16[5,48,1,128]{3,1,2,0:T(8,128)(2,1)S(1)}, bf16[5,48,1,128]{3,1,2,0:T(8,128)(2,1)S(1)}, u32[]{:S(2)}, u32[]{:S(2)}) collective-permute-start(bf16[5,48,1,128]{3,1,2,0:T(8,128)(2,1)S(1)} %get-tuple-element.239), channel_id=1, source_target_pairs={{0,1},{1,2},{2,3},{3,4},{4,5},{5,6},{6,7},{7,8},{8,9},{9,10},{10,1... | collective-permute-start | bytes 184328 | tf_op jit(solution)/shard_map/ppermute | solution.py:25
  198.2 3.4 %collective-permute-start.14 = (bf16[5,48,1,128]{3,1,2,0:T(8,128)(2,1)S(1)}, bf16[5,48,1,128]{3,1,2,0:T(8,128)(2,1)S(1)}, u32[]{:S(2)}, u32[]{:S(2)}) collective-permute-start(bf16[5,48,1,128]{3,1,2,0:T(8,128)(2,1)S(1)} %get-tuple-element.240), channel_id=1, source_target_pairs={{1,0},{2,1},{3,2},{4,3},{5,4},{6,5},{7,6},{8,7},{9,8},{10,9},{11,1... | collective-permute-start | bytes 184328 | tf_op jit(solution)/shard_map/ppermute | solution.py:26
  203.2 5.0 %collective-permute-start.18 = (bf16[5,48,1,128]{3,1,0,2:T(8,128)(2,1)S(1)}, bf16[5,48,1,128]{3,1,0,2:T(8,128)(2,1)S(1)}, u32[]{:S(2)}, u32[]{:S(2)}) collective-permute-start(bf16[5,48,1,128]{3,1,0,2:T(8,128)(2,1)S(1)} %get-tuple-element.243), channel_id=1, source_target_pairs={{0,1},{1,2},{2,3},{3,4},{4,5},{5,6},{6,7},{7,8},{8,9},{9,10},{10,1... | collective-permute-start | bytes 184328 | tf_op jit(solution)/shard_map/ppermute | solution.py:25
  207.3 1.9 collective-permute-start.19
  209.2 5.7 %copy-start.1 = (f32[2,5,48,8,128]{4,3,2,1,0:T(8,128)S(1)}, f32[2,5,48,8,128]{4,3,2,1,0:T(8,128)}, u32[]{:S(2)}) copy-start(f32[2,5,48,8,128]{4,3,2,1,0:T(8,128)} %copy-done) | copy-start | bytes 5898244
  (11 other events, 22.6 us)
where the time goes:
time: 276 us; the launch traced here: 275 us
  blocking collectives  103 us (37%)
  other arithmetic  60 us (22%)
  local copies, waits for them, and re-layouts  52.3 us (19%)
  starting transfers between devices  30.8 us (11%)
  waiting for transfers between devices  24.5 us (9%)
  between operations  4.8 us (2%)
    psum x1, blocking collectives, on_device(): misfit_square = lax.psum(misfit_local, ('tm', 'space'))  52.7 us
    psum x1, blocking collectives, on_device(): observed = lax.psum(local_values, 'space')  50 us
    gather x3, local copies, waits for them, and re-layouts, on_device(): jnp.take_along_axis(flattened, local_index, axis=1)  34.9 us
    unnamed x20, other arithmetic  31.8 us
    ppermute x9, starting transfers between devices, extended(): before = lax.ppermute(last, axis, up)  14.7 us
    ppermute x2, waiting for transfers between devices, shifted(): return lax.ppermute(shard, axis, pairs)  13.5 us
    ppermute x9, starting transfers between devices, extended(): after = lax.ppermute(first, axis, down)  10.5 us
    ppermute x9, waiting for transfers between devices, extended(): before = lax.ppermute(last, axis, up)  7.4 us
  transfers between devices with their start and end apart: 20, of which 9 were waited for; matrix products, arithmetic and copies ran while one was open for 28% of the time, Pallas kernels for 0%

commit v1 on v0

--- a/solution.py
+++ b/solution.py
@@ -2,6 +2,7 @@
 import jax.numpy as jnp
 from jax import lax
 from jax.sharding import PartitionSpec as P
+from jax.lax import all_gather
 
 thermal_lin = 0.2
 thermal_quad = 0.02
@@ -148,7 +149,7 @@
     )
     flattened = increment[:, :2].reshape(subcount, 2 * levels * width * latitude)
     local_values = jnp.where(owned, jnp.take_along_axis(flattened, local_index, axis=1), 0.0)
-    observed = lax.psum(local_values, "space")
+    observed = all_gather(local_values, "space").sum(axis=0)
     sensor_residual = innovation - sensor_error * sensor_multiplier - observed
     sensor_next = sensor_multiplier + relaxation * sensor_residual
     misfit_local = jnp.sum(model_residual * model_residual) + jnp.sum(

time: 276 us -> 238 us (0.86)
  blocking collectives: 103 us -> 68.5 us
  starting transfers between devices: 30.8 us -> 22.3 us
  waiting for transfers between devices: 24.5 us -> 30.1 us
    psum x1 -> x0, blocking collectives: 50 us -> none  [on_device(): observed = lax.psum(local_values, 'space')]
    all_gather x0 -> x1, blocking collectives: none -> 19.8 us  [on_device(): observed = all_gather(local_values, 'space').sum(axis=0)]
    ppermute x9, starting transfers between devices: 14.7 us -> 7.36 us  [extended(): before = lax.ppermute(last, axis, up)]
    ppermute x2, waiting for transfers between devices: 13.5 us -> 20.4 us  [shifted(): return lax.ppermute(shard, axis, pairs)]
    psum x1, blocking collectives: 52.7 us -> 48.8 us  [on_device(): misfit_square = lax.psum(misfit_local, ('tm', 'space'))]
    unnamed x20 -> x21, other arithmetic: 31.8 us -> 31.9 us
  transfers between devices with their start and end apart: 20 -> 20, of which waited for: 9 -> 10; matrix products, arithmetic and copies ran while one was open for 28% -> 33% of each run, Pallas kernels for 0% -> 0%
where the time goes in v1:
time: 238 us
  blocking collectives  68.5 us (29%)
  other arithmetic  60.1 us (25%)
  local copies, waits for them, and re-layouts  52.1 us (22%)
  waiting for transfers between devices  30.1 us (13%)
  starting transfers between devices  22.3 us (9%)
  between operations  4.82 us (2%)
    psum x1, blocking collectives, on_device(): misfit_square = lax.psum(misfit_local, ('tm', 'space'))  48.8 us
    gather x3, local copies, waits for them, and re-layouts, on_device(): jnp.take_along_axis(flattened, local_index, axis=1)  34.9 us
    unnamed x21, other arithmetic  31.9 us
    ppermute x2, waiting for transfers between devices, shifted(): return lax.ppermute(shard, axis, pairs)  20.4 us
    all_gather x1, blocking collectives, on_device(): observed = all_gather(local_values, 'space').sum(axis=0)  19.8 us
    ppermute x9, starting transfers between devices, extended(): after = lax.ppermute(first, axis, down)  9.59 us
    ppermute x9, starting transfers between devices, extended(): before = lax.ppermute(last, axis, up)  7.36 us
    unnamed x51, local copies, waits for them, and re-layouts  6.66 us
  transfers between devices with their start and end apart: 20, of which 10 were waited for; matrix products, arithmetic and copies ran while one was open for 33% of the time, Pallas kernels for 0%

profile of v1, /device:TPU:12, one launch (start us, length us, event | category | flops | bytes accessed | tf_op | source)
XLA Modules:
  0.0 237.9 jit_solution(16596057230916992848)
XLA Ops:
  0.6 1.9 copy.52
  4.5 1.7 collective-permute-start.1
  7.2 2.6 %collective-permute-start.2 = (bf16[2,2,2,48,1,128]{5,3,4,2,1,0:T(8,128)(2,1)S(1)}, bf16[2,2,2,48,1,128]{5,3,4,2,1,0:T(8,128)(2,1)S(1)}, u32[]{:S(2)}, u32[]{:S(2)}) collective-permute-start(bf16[2,2,2,48,1,128]{5,3,4,2,1,0:T(8,128)(2,1)S(1)} %get-tuple-element.237), channel_id=1, source_target_pairs={{0,1},{1,2},{2,3},{3,4},{4,5},{5,6},{6,7},{7,8},{8,9},{9,10},{10,1... | collective-permute-start | bytes 294920 | tf_op jit(solution)/shard_map/ppermute | solution.py:26
  10.7 34.9 %gather_fusion = f32[4096]{0:T(1024)S(1)} fusion(f32[2,98304]{1,0:T(2,128)S(1)} %bitcast.528, s32[4096]{0:T(1024)S(1)} %bitcast.529), kind=kCustom, calls=%fused_computation | custom fusion | bytes 65536 | tf_op jit(solution)/shard_map/jit(take_along_axis)/gather | solution.py:151
  45.7 19.8 %all-gather.1 = f32[16,2,2048]{2,1,0:T(2,128)S(1)} all-gather(f32[1,2,2048]{2,1,0:T(2,128)S(1)} %fusion.204), channel_id=2, replica_groups=mesh['tm'=2,'space'=16] {'space'}, dimensions={0}, use_global_device_ids=true | all-gather | bytes 278528 | tf_op jit(solution)/shard_map/all_gather | solution.py:152
  65.6 1.3 select_bitcast_fusion.1
  67.1 27.9 %scatter_custom_fusion = f32[196608]{0:T(1024)} fusion(s32[4096]{0:T(1024)S(1)} %bitcast.543, f32[4096]{0:T(1024)S(1)} %bitcast.542, f32[]{:T(128)} %constant.307.clone.1), kind=kCustom, calls=%fused_computation.80 | custom fusion | flops 4096 | bytes 786436
  101.8 2.9 %collective-permute-start.4 = (f32[5,48,1,128]{3,1,2,0:T(8,128)S(1)}, f32[5,48,1,128]{3,1,2,0:T(8,128)S(1)}, u32[]{:S(2)}, u32[]{:S(2)}) collective-permute-start(f32[5,48,1,128]{3,1,2,0:T(8,128)S(1)} %get-tuple-element.229), channel_id=1, source_target_pairs={{0,1},{1,2},{2,3},{3,4},{4,5},{5,6},{6,7},{7,8},{8,9},{9,10},{10,1... | collective-permute-start | bytes 368648 | tf_op jit(solution)/shard_map/ppermute | solution.py:26
  104.7 1.9 collective-permute-start.10
  107.4 2.9 %collective-permute-done.10 = f32[5,48,1,128]{3,1,2,0:T(8,128)S(1)} collective-permute-done((f32[5,48,1,128]{3,1,2,0:T(8,128)S(1)}, f32[5,48,1,128]{3,1,2,0:T(8,128)S(1)}, u32[]{:S(2)}, u32[]{:S(2)}) %collective-permute-start.10) | collective-permute-done | bytes 122912 | tf_op jit(solution)/shard_map/ppermute | solution.py:27
  110.3 2.5 %collective-permute-done.9 = f32[5,48,1,128]{3,1,2,0:T(8,128)S(1)} collective-permute-done((f32[5,48,1,128]{3,1,2,0:T(8,128)S(1)}, f32[5,48,1,128]{3,1,2,0:T(8,128)S(1)}, u32[]{:S(2)}, u32[]{:S(2)}) %collective-permute-start.9) | collective-permute-done | bytes 122912 | tf_op jit(solution)/shard_map/ppermute | solution.py:26
  114.3 4.0 %collective-permute-start.6 = (bf16[5,48,8,128]{3,1,2,0:T(8,128)(2,1)S(1)}, bf16[5,48,8,128]{3,1,2,0:T(8,128)(2,1)S(1)}, u32[]{:S(2)}, u32[]{:S(2)}) collective-permute-start(bf16[5,48,8,128]{3,1,2,0:T(8,128)(2,1)S(1)} %multiply_convert_fusion), channel_id=1, source_target_pairs={{0,16},{1,17},{2,18},{3,19},{4,20},{5,21},{6,22},{7,23},{8,24},{9,... | collective-permute-start | bytes 1474568 | tf_op jit(solution)/shard_map/ppermute | solution.py:35
  119.4 7.9 %collective-permute-done.6 = bf16[5,48,8,128]{3,1,2,0:T(8,128)(2,1)S(1)} collective-permute-done((bf16[5,48,8,128]{3,1,2,0:T(8,128)(2,1)S(1)}, bf16[5,48,8,128]{3,1,2,0:T(8,128)(2,1)S(1)}, u32[]{:S(2)}, u32[]{:S(2)}) %collective-permute-start.6) | collective-permute-done | bytes 491552 | tf_op jit(solution)/shard_map/ppermute | solution.py:35
  127.5 1.6 broadcast_multiply_fusion
  131.6 1.4 copy-done.4
  133.0 1.2 fusion.5
  134.3 1.3 collective-permute-start.15
  137.1 1.7 collective-permute-start.12
  138.8 1.2 multiply_reduce_fusion.1
  142.3 1.6 fusion.200
  143.9 1.6 fusion.199
  145.5 12.5 %collective-permute-done.15 = f32[5,48,8,128]{3,1,2,0:T(8,128)} collective-permute-done((f32[5,48,8,128]{3,1,2,0:T(8,128)}, f32[5,48,8,128]{3,1,2,0:T(8,128)}, u32[]{:S(2)}, u32[]{:S(2)}) %collective-permute-start.15) | collective-permute-done | bytes 983072 | tf_op jit(solution)/shard_map/ppermute | solution.py:35
  158.0 1.7 broadcast_multiply_fusion.3
  163.4 1.7 collective-permute-start.17
  165.7 1.7 collective-permute-start.14
  171.3 1.7 collective-permute-start.18
  173.9 1.4 collective-permute-done.18
  175.9 1.3 copy.59
  177.3 4.4 %scatter-add.54 = f32[1,5,48,8,128]{4,3,2,1,0:T(8,128)} dynamic-update-slice(f32[1,5,48,8,128]{4,3,2,1,0:T(8,128)} %copy.59, f32[1,5,48,1,128]{4,3,2,1,0:T(1,128)S(1)} %bitcast.539, s32[]{:T(128)} %constant.322.clone.1, s32[]{:T(128)} %constant.322.clone.1, s32[]{:T(128)} %constant.322.clone.1, s32[]{:T(128)} %constant.327.clone.1, s32[]{:T(128)} %constant.322.clone.1) | dynamic-update-slice | bytes 245764 | tf_op jit(solution)/shard_map/scatter-add | solution.py:101
  181.6 2.6 %multiply_reduce_fusion = f32[]{:T(128)} fusion(f32[2,2,48,8,128]{4,3,2,1,0:T(8,128)} %bitcast.531, f32[2,5,48,8,128]{4,3,2,1,0:T(8,128)S(1)} %copy-done.1, f32[1,5,48,8,128]{4,3,2,1,0:T(8,128)} %scatter-add.54, f32[1,5,48,8,128]{4,3,2,1,0:T(8,128)S(1)} %copy.60), kind=kLoop, calls=%fused_computation.8 | loop fusion | flops 2457599 | bytes 4718596 | tf_op jit(solution)/shard_map/reduce_sum | solution.py:180
  184.2 48.8 %all-reduce.221 = (f32[]{:T(128)}, f32[]{:T(128)}) all-reduce(f32[]{:T(128)S(6)} %add.908, f32[]{:T(128)} %multiply_reduce_fusion), channel_id=1, replica_groups=mesh['tm'=2,'space'=16] {'tm','space'}, use_global_device_ids=true, to_apply=%region_3.4 | all-reduce | flops 2 | bytes 16 | tf_op jit(solution)/shard_map/psum | solution.py:158
  234.2 3.6 %multiply_subtract_fusion = f32[2,5,48,8,128]{4,3,2,1,0:T(8,128)} fusion(f32[2,5,48,8,128]{4,3,2,1,0:T(8,128)} %param.26, f32[]{:T(128)S(6)} %div.69, f32[2,2,48,8,128]{4,3,2,1,0:T(8,128)} %bitcast.532, f32[2,5,48,8,128]{4,3,2,1,0:T(8,128)S(1)} %copy-done.1, f32[1,5,48,8,128]{4,3,2,1,0:T(8,128)} %scatter-add.54, f32[1,5,48,8,128]{4,3,2,1,0:T(8,128)S(1)} %copy.60), kind=kLoop, calls=%fused_computation.7 | loop fusion | flops 2457600 | bytes 8650756 | tf_op jit(solution)/shard_map/sub | solution.py:183
  (252 shorter events, 27.8 us)
Async XLA Ops:
  3.8 3.3 %copy-start.8 = (f32[5,48,8,128]{3,1,2,0:T(8,128)}, f32[5,48,8,128]{3,1,2,0:T(8,128)S(1)}, u32[]{:S(2)}) copy-start(f32[5,48,8,128]{3,1,2,0:T(8,128)S(1)} %get-tuple-element.131) | copy-start | bytes 2949124
  4.5 92.3 %collective-permute-start = (f32[5,48,1,128]{3,1,2,0:T(8,128)}, f32[5,48,1,128]{3,1,2,0:T(8,128)}, u32[]{:S(2)}, u32[]{:S(2)}) collective-permute-start(f32[5,48,1,128]{3,1,2,0:T(8,128)} %get-tuple-element.231), channel_id=1, source_target_pairs={{0,1},{1,2},{2,3},{3,4},{4,5},{5,6},{6,7},{7,8},{8,9},{9,10},{10,1... | collective-permute-start | bytes 368648 | tf_op jit(solution)/shard_map/ppermute | solution.py:26
  4.5 92.3 %collective-permute-start.1 = (f32[5,48,1,128]{3,1,2,0:T(8,128)}, f32[5,48,1,128]{3,1,2,0:T(8,128)}, u32[]{:S(2)}, u32[]{:S(2)}) collective-permute-start(f32[5,48,1,128]{3,1,2,0:T(8,128)} %get-tuple-element.232), channel_id=1, source_target_pairs={{1,0},{2,1},{3,2},{4,3},{5,4},{6,5},{7,6},{8,7},{9,8},{10,9},{11,1... | collective-permute-start | bytes 368648 | tf_op jit(solution)/shard_map/ppermute | solution.py:27
  7.0 91.0 %collective-permute-start.7 = (f32[5,48,1,128]{3,1,2,0:T(8,128)}, f32[5,48,1,128]{3,1,2,0:T(8,128)}, u32[]{:S(2)}, u32[]{:S(2)}) collective-permute-start(f32[5,48,1,128]{3,1,2,0:T(8,128)} %get-tuple-element.235), channel_id=1, source_target_pairs={{0,1},{1,2},{2,3},{3,4},{4,5},{5,6},{6,7},{7,8},{8,9},{9,10},{10,1... | collective-permute-start | bytes 368648 | tf_op jit(solution)/shard_map/ppermute | solution.py:26
  7.2 87.9 %collective-permute-start.2 = (bf16[2,2,2,48,1,128]{5,3,4,2,1,0:T(8,128)(2,1)S(1)}, bf16[2,2,2,48,1,128]{5,3,4,2,1,0:T(8,128)(2,1)S(1)}, u32[]{:S(2)}, u32[]{:S(2)}) collective-permute-start(bf16[2,2,2,48,1,128]{5,3,4,2,1,0:T(8,128)(2,1)S(1)} %get-tuple-element.237), channel_id=1, source_target_pairs={{0,1},{1,2},{2,3},{3,4},{4,5},{5,6},{6,7},{7,8},{8,9},{9,10},{10,1... | collective-permute-start | bytes 294920 | tf_op jit(solution)/shard_map/ppermute | solution.py:26
  9.8 86.0 %collective-permute-start.3 = (bf16[2,2,2,48,1,128]{5,3,4,2,1,0:T(8,128)(2,1)S(1)}, bf16[2,2,2,48,1,128]{5,3,4,2,1,0:T(8,128)(2,1)}, u32[]{:S(2)}, u32[]{:S(2)}) collective-permute-start(bf16[2,2,2,48,1,128]{5,3,4,2,1,0:T(8,128)(2,1)S(1)} %get-tuple-element.238), channel_id=1, source_target_pairs={{1,0},{2,1},{3,2},{4,3},{5,4},{6,5},{7,6},{8,7},{9,8},{10,9},{11,1... | collective-permute-start | bytes 294920 | tf_op jit(solution)/shard_map/ppermute | solution.py:27
  10.6 54.9 %copy-start.15 = (f32[2,2048]{1,0:T(2,128)S(1)}, f32[2,2048]{1,0:T(2,128)}, u32[]{:S(2)}) copy-start(f32[2,2048]{1,0:T(2,128)} %param.28) | copy-start | bytes 49156
  10.7 54.9 %copy-start.16 = (f32[2,2048]{1,0:T(2,128)S(1)}, f32[2,2048]{1,0:T(2,128)}, u32[]{:S(2)}) copy-start(f32[2,2048]{1,0:T(2,128)} %param.30) | copy-start | bytes 49156
  10.7 54.9 %copy-start.17 = (f32[2,2048]{1,0:T(2,128)S(1)}, f32[2,2048]{1,0:T(2,128)}, u32[]{:S(2)}) copy-start(f32[2,2048]{1,0:T(2,128)} %param.32) | copy-start | bytes 49156
  10.7 56.2 %copy-start.20 = (s32[2]{0:T(128)S(1)}, s32[2]{0:T(128)}, u32[]{:S(2)}) copy-start(s32[2]{0:T(128)} %constant.788) | copy-start | bytes 28
  10.7 56.3 %copy-start.21 = (s32[2]{0:T(128)S(1)}, s32[2]{0:T(128)}, u32[]{:S(2)}) copy-start(s32[2]{0:T(128)} %constant.791) | copy-start | bytes 28
  95.1 3.1 %collective-permute-start.8 = (f32[5,48,1,128]{3,1,2,0:T(8,128)}, f32[5,48,1,128]{3,1,2,0:T(8,128)S(1)}, u32[]{:S(2)}, u32[]{:S(2)}) collective-permute-start(f32[5,48,1,128]{3,1,2,0:T(8,128)} %get-tuple-element.236), channel_id=1, source_target_pairs={{1,0},{2,1},{3,2},{4,3},{5,4},{6,5},{7,6},{8,7},{9,8},{10,9},{11,1... | collective-permute-start | bytes 368648 | tf_op jit(solution)/shard_map/ppermute | solution.py:27
  101.8 4.7 %collective-permute-start.4 = (f32[5,48,1,128]{3,1,2,0:T(8,128)S(1)}, f32[5,48,1,128]{3,1,2,0:T(8,128)S(1)}, u32[]{:S(2)}, u32[]{:S(2)}) collective-permute-start(f32[5,48,1,128]{3,1,2,0:T(8,128)S(1)} %get-tuple-element.229), channel_id=1, source_target_pairs={{0,1},{1,2},{2,3},{3,4},{4,5},{5,6},{6,7},{7,8},{8,9},{9,10},{10,1... | collective-permute-start | bytes 368648 | tf_op jit(solution)/shard_map/ppermute | solution.py:26
  104.7 2.4 %collective-permute-start.5 = (f32[5,48,1,128]{3,1,2,0:T(8,128)S(1)}, f32[5,48,1,128]{3,1,2,0:T(8,128)S(1)}, u32[]{:S(2)}, u32[]{:S(2)}) collective-permute-start(f32[5,48,1,128]{3,1,2,0:T(8,128)S(1)} %get-tuple-element.230), channel_id=1, source_target_pairs={{1,0},{2,1},{3,2},{4,3},{5,4},{6,5},{7,6},{8,7},{9,8},{10,9},{11,1... | collective-permute-start | bytes 368648 | tf_op jit(solution)/shard_map/ppermute | solution.py:27
  104.7 5.6 %collective-permute-start.10 = (f32[5,48,1,128]{3,1,2,0:T(8,128)S(1)}, f32[5,48,1,128]{3,1,2,0:T(8,128)S(1)}, u32[]{:S(2)}, u32[]{:S(2)}) collective-permute-start(f32[5,48,1,128]{3,1,2,0:T(8,128)S(1)} %get-tuple-element.234), channel_id=1, source_target_pairs={{1,0},{2,1},{3,2},{4,3},{5,4},{6,5},{7,6},{8,7},{9,8},{10,9},{11,1... | collective-permute-start | bytes 368648 | tf_op jit(solution)/shard_map/ppermute | solution.py:27
  106.6 6.2 %collective-permute-start.9 = (f32[5,48,1,128]{3,1,2,0:T(8,128)S(1)}, f32[5,48,1,128]{3,1,2,0:T(8,128)S(1)}, u32[]{:S(2)}, u32[]{:S(2)}) collective-permute-start(f32[5,48,1,128]{3,1,2,0:T(8,128)S(1)} %get-tuple-element.233), channel_id=1, source_target_pairs={{0,1},{1,2},{2,3},{3,4},{4,5},{5,6},{6,7},{7,8},{8,9},{9,10},{10,1... | collective-permute-start | bytes 368648 | tf_op jit(solution)/shard_map/ppermute | solution.py:26
  114.3 13.1 %collective-permute-start.6 = (bf16[5,48,8,128]{3,1,2,0:T(8,128)(2,1)S(1)}, bf16[5,48,8,128]{3,1,2,0:T(8,128)(2,1)S(1)}, u32[]{:S(2)}, u32[]{:S(2)}) collective-permute-start(bf16[5,48,8,128]{3,1,2,0:T(8,128)(2,1)S(1)} %multiply_convert_fusion), channel_id=1, source_target_pairs={{0,16},{1,17},{2,18},{3,19},{4,20},{5,21},{6,22},{7,23},{8,24},{9,... | collective-permute-start | bytes 1474568 | tf_op jit(solution)/shard_map/ppermute | solution.py:35
  118.8 8.6 %copy-start.11 = (f32[2,5,48,8,128]{4,3,2,1,0:T(8,128)S(1)}, f32[2,5,48,8,128]{4,3,2,1,0:T(8,128)}, u32[]{:S(2)}) copy-start(f32[2,5,48,8,128]{4,3,2,1,0:T(8,128)} %param.29) | copy-start | bytes 5898244
  119.0 8.4 %copy-start.5 = (f32[2,5,48,8,128]{4,3,2,1,0:T(8,128)S(1)}, f32[2,5,48,8,128]{4,3,2,1,0:T(8,128)}, u32[]{:S(2)}) copy-start(f32[2,5,48,8,128]{4,3,2,1,0:T(8,128)} %param.27) | copy-start | bytes 5898244
  119.3 8.1 %copy-start.2 = (f32[2,5,48,8,128]{4,3,2,1,0:T(8,128)S(1)}, f32[2,5,48,8,128]{4,3,2,1,0:T(8,128)}, u32[]{:S(2)}) copy-start(f32[2,5,48,8,128]{4,3,2,1,0:T(8,128)} %param.26) | copy-start | bytes 5898244
  119.4 8.0 %copy-start.14 = (f32[5,48]{1,0:T(8,128)S(1)}, f32[5,48]{1,0:T(8,128)}, u32[]{:S(2)}) copy-start(f32[5,48]{1,0:T(8,128)} %param.31) | copy-start | bytes 2884
  134.3 23.7 %collective-permute-start.15 = (f32[5,48,8,128]{3,1,2,0:T(8,128)}, f32[5,48,8,128]{3,1,2,0:T(8,128)}, u32[]{:S(2)}, u32[]{:S(2)}) collective-permute-start(f32[5,48,8,128]{3,1,2,0:T(8,128)} %fusion.5), channel_id=1, source_target_pairs={{16,0},{17,1},{18,2},{19,3},{20,4},{21,5},{22,6},{23,7},{24,8},{25... | collective-permute-start | bytes 2949128 | tf_op jit(solution)/shard_map/ppermute | solution.py:35
  137.0 4.0 %copy-start.10 = (f32[5,48,10,128]{3,1,2,0:T(8,128)}, f32[5,48,10,128]{3,1,2,0:T(8,128)S(1)}, u32[]{:S(2)}) copy-start(f32[5,48,10,128]{3,1,2,0:T(8,128)S(1)} %get-tuple-element.106) | copy-start | bytes 3686404
  137.0 5.3 %collective-permute-start.11 = (bf16[5,48,1,128]{3,1,2,0:T(8,128)(2,1)S(1)}, bf16[5,48,1,128]{3,1,2,0:T(8,128)(2,1)S(1)}, u32[]{:S(2)}, u32[]{:S(2)}) collective-permute-start(bf16[5,48,1,128]{3,1,2,0:T(8,128)(2,1)S(1)} %get-tuple-element.241), channel_id=1, source_target_pairs={{0,1},{1,2},{2,3},{3,4},{4,5},{5,6},{6,7},{7,8},{8,9},{9,10},{10,1... | collective-permute-start | bytes 184328 | tf_op jit(solution)/shard_map/ppermute | solution.py:26
  137.1 5.3 %collective-permute-start.12 = (bf16[5,48,1,128]{3,1,2,0:T(8,128)(2,1)S(1)}, bf16[5,48,1,128]{3,1,2,0:T(8,128)(2,1)S(1)}, u32[]{:S(2)}, u32[]{:S(2)}) collective-permute-start(bf16[5,48,1,128]{3,1,2,0:T(8,128)(2,1)S(1)} %get-tuple-element.242), channel_id=1, source_target_pairs={{1,0},{2,1},{3,2},{4,3},{5,4},{6,5},{7,6},{8,7},{9,8},{10,9},{11,1... | collective-permute-start | bytes 184328 | tf_op jit(solution)/shard_map/ppermute | solution.py:27
  163.3 4.2 %collective-permute-start.16 = (bf16[5,48,1,128]{3,1,2,0:T(8,128)(2,1)S(1)}, bf16[5,48,1,128]{3,1,2,0:T(8,128)(2,1)S(1)}, u32[]{:S(2)}, u32[]{:S(2)}) collective-permute-start(bf16[5,48,1,128]{3,1,2,0:T(8,128)(2,1)S(1)} %get-tuple-element.245), channel_id=1, source_target_pairs={{0,1},{1,2},{2,3},{3,4},{4,5},{5,6},{6,7},{7,8},{8,9},{9,10},{10,1... | collective-permute-start | bytes 184328 | tf_op jit(solution)/shard_map/ppermute | solution.py:26
  163.4 4.1 %collective-permute-start.17 = (bf16[5,48,1,128]{3,1,2,0:T(8,128)(2,1)S(1)}, bf16[5,48,1,128]{3,1,2,0:T(8,128)(2,1)S(1)}, u32[]{:S(2)}, u32[]{:S(2)}) collective-permute-start(bf16[5,48,1,128]{3,1,2,0:T(8,128)(2,1)S(1)} %get-tuple-element.246), channel_id=1, source_target_pairs={{1,0},{2,1},{3,2},{4,3},{5,4},{6,5},{7,6},{8,7},{9,8},{10,9},{11,1... | collective-permute-start | bytes 184328 | tf_op jit(solution)/shard_map/ppermute | solution.py:27
  165.6 3.7 %collective-permute-start.13 = (bf16[5,48,1,128]{3,1,2,0:T(8,128)(2,1)S(1)}, bf16[5,48,1,128]{3,1,2,0:T(8,128)(2,1)S(1)}, u32[]{:S(2)}, u32[]{:S(2)}) collective-permute-start(bf16[5,48,1,128]{3,1,2,0:T(8,128)(2,1)S(1)} %get-tuple-element.239), channel_id=1, source_target_pairs={{0,1},{1,2},{2,3},{3,4},{4,5},{5,6},{6,7},{7,8},{8,9},{9,10},{10,1... | collective-permute-start | bytes 184328 | tf_op jit(solution)/shard_map/ppermute | solution.py:26
  165.7 4.0 %collective-permute-start.14 = (bf16[5,48,1,128]{3,1,2,0:T(8,128)(2,1)S(1)}, bf16[5,48,1,128]{3,1,2,0:T(8,128)(2,1)S(1)}, u32[]{:S(2)}, u32[]{:S(2)}) collective-permute-start(bf16[5,48,1,128]{3,1,2,0:T(8,128)(2,1)S(1)} %get-tuple-element.240), channel_id=1, source_target_pairs={{1,0},{2,1},{3,2},{4,3},{5,4},{6,5},{7,6},{8,7},{9,8},{10,9},{11,1... | collective-permute-start | bytes 184328 | tf_op jit(solution)/shard_map/ppermute | solution.py:27
  171.3 4.1 %collective-permute-start.18 = (bf16[5,48,1,128]{3,1,0,2:T(8,128)(2,1)S(1)}, bf16[5,48,1,128]{3,1,0,2:T(8,128)(2,1)S(1)}, u32[]{:S(2)}, u32[]{:S(2)}) collective-permute-start(bf16[5,48,1,128]{3,1,0,2:T(8,128)(2,1)S(1)} %get-tuple-element.243), channel_id=1, source_target_pairs={{0,1},{1,2},{2,3},{3,4},{4,5},{5,6},{6,7},{7,8},{8,9},{9,10},{10,1... | collective-permute-start | bytes 184328 | tf_op jit(solution)/shard_map/ppermute | solution.py:26
  173.0 2.9 %collective-permute-start.19 = (bf16[5,48,1,128]{3,1,0,2:T(8,128)(2,1)S(1)}, bf16[5,48,1,128]{3,1,0,2:T(8,128)(2,1)S(1)}, u32[]{:S(2)}, u32[]{:S(2)}) collective-permute-start(bf16[5,48,1,128]{3,1,0,2:T(8,128)(2,1)S(1)} %get-tuple-element.244), channel_id=1, source_target_pairs={{1,0},{2,1},{3,2},{4,3},{5,4},{6,5},{7,6},{8,7},{9,8},{10,9},{11,1... | collective-permute-start | bytes 184328 | tf_op jit(solution)/shard_map/ppermute | solution.py:27
  175.9 5.7 %copy-start.1 = (f32[2,5,48,8,128]{4,3,2,1,0:T(8,128)S(1)}, f32[2,5,48,8,128]{4,3,2,1,0:T(8,128)}, u32[]{:S(2)}) copy-start(f32[2,5,48,8,128]{4,3,2,1,0:T(8,128)} %copy-done) | copy-start | bytes 5898244
  (11 other events, 22.6 us)
